TPU v7x, 32 devices: a whole 2x2x4 slice. The times are simulated.
32 devices in a mesh: seq: 4 (over z), exp: 2 (over core), hid: 4 (over y, x).
Axes of the slice: x: 2, y: 2, z: 4, core: 2. Of those that a mesh axis runs over, the one named last changes fastest.
Arguments:
- tokens: bfloat16 [512, 6144], P('seq'), may hold values from -6 to 6
- out_grad: bfloat16 [512, 6144], P('seq'), may hold values from -3 to 3
- expert_ids: int32 [512, 2], P('seq'), may hold values from 0 to 7, as said below
- gate_probs: float32 [512, 2], P('seq'), may hold values from 0.1 to 1
- w_gate: bfloat16 [2, 6144, 16384], P('exp', None, ('seq', 'hid')), may hold values from -0.078125 to 0.078125
- w_up: bfloat16 [2, 6144, 16384], P('exp', None, ('seq', 'hid')), may hold values from -0.078125 to 0.078125
- w_down: bfloat16 [2, 16384, 6144], P('exp', ('seq', 'hid')), may hold values from -0.046875 to 0.046875
Outputs:
- d_w_gate: bfloat16 [2, 6144, 16384], P('exp', None, ('seq', 'hid'))
- d_w_up: bfloat16 [2, 6144, 16384], P('exp', None, ('seq', 'hid'))
- d_w_down: bfloat16 [2, 16384, 6144], P('exp', ('seq', 'hid'))
- d_tokens: float32 [512, 6144], P('seq', 'hid')
- d_gates: float32 [512, 2], P('seq')
Inputs may be any that keep to these rules, and one draw needn't show every extreme that they name: `expert_ids`: in each block of 128 rows (the tokens of one index of seq) the two ids of a row differ and no expert is named more than 40 times; each expert below 2 is named 40 // 2 to 40 times in a block, exactly 40 times in the first block.
All inputs are finite; a program needn't handle non-finite values.
Results may differ from a plain program's by a relative error of at most 0.015.
Values may be sent and summed in bfloat16 or wider, within the bound.
No kernel may reach another device: no remote copies, remote signals or barrier semaphores. Data moves between devices by JAX's collectives and lax.ppermute only.
A program may use at most 192 MiB of HBM per device.

v0:
```python
import jax
import jax.numpy as jnp
from jax import lax
from jax.sharding import PartitionSpec as P


def on_device(tokens, out_grad, expert_ids, gate_probs, w_gate, w_up, w_down):
    expert = lax.axis_index("exp")
    tok_rows = tokens.shape[0]
    model_width = tokens.shape[1]
    capacity = 5 * tok_rows // 16
    seq_count = lax.axis_size("seq")
    hid_count = lax.axis_size("hid")
    piece_width = model_width // hid_count
    hidden_local = w_gate.shape[2]
    chosen = (expert_ids == expert).astype(jnp.int32)
    slot_index = (jnp.cumsum(chosen.reshape(-1)) - 1).reshape(tok_rows, 2)
    columns = jnp.arange(capacity, dtype=jnp.int32)
    pick_table = (
        (chosen[:, :, None] == 1) & (slot_index[:, :, None] == columns[None, None, :])
    ).astype(jnp.float32)
    select_rows = jnp.sum(pick_table, axis=1)
    select_half = select_rows.astype(jnp.bfloat16)
    contract_rows = (((0,), (0,)), ((), ()))
    token_slots = lax.dot_general(
        select_half, tokens, contract_rows, preferred_element_type=jnp.float32
    ).astype(jnp.bfloat16)
    grad_slots = lax.dot_general(
        select_half, out_grad, contract_rows, preferred_element_type=jnp.float32
    ).astype(jnp.bfloat16)
    weight_slots = jnp.sum(pick_table * gate_probs[:, :, None], axis=(0, 1))
    rows_e, grads_e, weight_e = (
        lax.all_gather(token_slots, "seq", axis=0, tiled=True),
        lax.all_gather(grad_slots, "seq", axis=0, tiled=True),
        lax.all_gather(weight_slots.astype(jnp.bfloat16), "seq", axis=0, tiled=True).astype(
            weight_slots.dtype
        ),
    )
    gate_mat = w_gate[0]
    up_mat = w_up[0]
    down_mat = w_down[0]
    gate_pre = jnp.dot(rows_e, gate_mat, preferred_element_type=jnp.float32)
    up_pre = jnp.dot(rows_e, up_mat, preferred_element_type=jnp.float32)
    sig_gate = jax.nn.sigmoid(gate_pre)
    activated = gate_pre * sig_gate
    hidden = (activated * up_pre).astype(jnp.bfloat16)
    back_hidden = lax.dot_general(
        grads_e, down_mat, (((1,), (1,)), ((), ())), preferred_element_type=jnp.float32
    )
    slot_part = jnp.sum(hidden.astype(jnp.float32) * back_hidden, axis=1)
    weighted = (weight_e[:, None] * hidden.astype(jnp.float32)).astype(jnp.bfloat16)
    grad_down = lax.dot_general(
        weighted, grads_e, contract_rows, preferred_element_type=jnp.float32
    ).astype(jnp.bfloat16)
    scaled_back = weight_e[:, None] * back_hidden
    d_gate = (scaled_back * up_pre * (sig_gate * (1.0 + gate_pre * (1.0 - sig_gate)))).astype(
        jnp.bfloat16
    )
    d_up = (scaled_back * activated).astype(jnp.bfloat16)
    grad_gate = lax.dot_general(
        rows_e, d_gate, contract_rows, preferred_element_type=jnp.float32
    ).astype(jnp.bfloat16)
    grad_up = lax.dot_general(
        rows_e, d_up, contract_rows, preferred_element_type=jnp.float32
    ).astype(jnp.bfloat16)
    gate_blocks = d_gate.reshape(seq_count, capacity, hidden_local)
    up_blocks = d_up.reshape(seq_count, capacity, hidden_local)
    partials = jnp.einsum(
        "sqf,hcf->shqc",
        gate_blocks,
        gate_mat.reshape(hid_count, piece_width, hidden_local),
        preferred_element_type=jnp.float32,
    )
    partials = partials + jnp.einsum(
        "sqf,hcf->shqc",
        up_blocks,
        up_mat.reshape(hid_count, piece_width, hidden_local),
        preferred_element_type=jnp.float32,
    )
    slot_terms = jnp.broadcast_to(
        slot_part.reshape(seq_count, 1, capacity), (seq_count, hid_count, capacity)
    )
    flat_parts = partials.reshape(seq_count * hid_count, capacity, piece_width)
    flat_slots = slot_terms.reshape(seq_count * hid_count, capacity)
    partials, slot_terms = (
        lax.psum_scatter(flat_parts, ("seq", "hid"), scatter_dimension=0, tiled=True),
        lax.psum_scatter(flat_slots, ("seq", "hid"), scatter_dimension=0, tiled=True),
    )
    own_rows = partials.reshape(capacity, piece_width)
    slot_grad = slot_terms.reshape(capacity)
    token_part = jnp.dot(
        select_rows, own_rows, precision=lax.Precision.HIGHEST, preferred_element_type=jnp.float32
    )
    gate_part = jnp.sum(pick_table * slot_grad[None, None, :], axis=2)
    token_sum, gate_sum = (
        lax.psum(token_part.astype(jnp.bfloat16), "exp").astype(jnp.float32),
        lax.psum(gate_part.astype(jnp.bfloat16), "exp").astype(jnp.float32),
    )
    return (grad_gate[None], grad_up[None], grad_down[None], token_sum, gate_sum)


def solution(mesh):
    return jax.shard_map(
        on_device,
        mesh=mesh,
        in_specs=(
            P("seq", None),
            P("seq", None),
            P("seq", None),
            P("seq", None),
            P("exp", None, ("seq", "hid")),
            P("exp", None, ("seq", "hid")),
            P("exp", ("seq", "hid"), None),
        ),
        out_specs=(
            P("exp", None, ("seq", "hid")),
            P("exp", None, ("seq", "hid")),
            P("exp", ("seq", "hid"), None),
            P("seq", "hid"),
            P("seq", None),
        ),
        check_vma=False,
    )
```

profile of v0, /device:TPU:0, one launch (start us, length us, event | category | flops | bytes accessed | tf_op | source)
XLA Modules:
  0.0 344.5 jit_solution(5438517381305366996)
XLA Ops:
  7.3 0.8 broadcast_compare_fusion
  8.0 0.1 copy.22
  8.2 0.1 reshape.70
  8.3 0.3 reduce-window.9
  8.6 0.1 reshape.71
  8.9 0.1 slice_reduce_fusion
  9.3 1.1 convolution_convert_fusion.1
  10.5 2.5 convolution_convert_fusion
  13.1 0.6 dynamic-slice.1
  13.7 0.6 dynamic-slice
  14.9 41.9 %all-gather.3.cloned.1.call-done = bf16[160,6144]{1,0:T(8,128)(2,1)} async-done(((bf16[40,6144]{1,0:T(8,128)(2,1)}), bf16[160,6144]{1,0:T(8,128)(2,1)}) %all-gather.3.cloned.1.call-update) | async-done | bytes 1966096 | tf_op jit(solution)/shard_map/all_gather | solution.py:33
  56.8 7.5 %fusion = f32[160,1024]{1,0:T(8,128)S(1)} fusion(bf16[160,6144]{1,0:T(8,128)(2,1)} %all-gather.3.cloned.1.call-done, bf16[1,6144,1024]{2,1,0:T(8,128)(2,1)} %param.11), kind=kOutput, calls=%fused_computation | convolution fusion | flops 2013265920 | bytes 15204352 | tf_op jit(solution)/shard_map/dot_general | solution.py:42
  64.4 7.1 %fusion.2 = f32[160,1024]{1,0:T(8,128)S(1)} fusion(bf16[160,6144]{1,0:T(8,128)(2,1)S(1)} %copy-done.2, bf16[1,6144,1024]{2,1,0:T(8,128)(2,1)} %param.12), kind=kOutput, calls=%fused_computation.2 | convolution fusion | flops 2013265920 | bytes 15204352 | tf_op jit(solution)/shard_map/dot_general | solution.py:43
  71.5 29.9 %all-gather.5.cloned.1.call-done = bf16[160,6144]{1,0:T(8,128)(2,1)} async-done(((bf16[40,6144]{1,0:T(8,128)(2,1)}), bf16[160,6144]{1,0:T(8,128)(2,1)}) %all-gather.5.cloned.1.call-update) | async-done | bytes 1966096 | tf_op jit(solution)/shard_map/all_gather | solution.py:34
  101.4 10.4 %fusion.7 = (f32[160]{0:T(256)S(1)}, bf16[160,1024]{1,0:T(8,128)(2,1)}, f32[160,1024]{1,0:T(8,128)}) fusion(f32[160,1024]{1,0:T(8,128)S(1)} %fusion.2, f32[160,1024]{1,0:T(8,128)S(1)} %fusion, bf16[160,6144]{1,0:T(8,128)(2,1)} %all-gather.5.cloned.1.call-done, bf16[1,1024,6144]{2,1,0:T(8,128)(2,1)} %param.13), kind=kOutput, calls=%fused_computation.16 | convolution fusion | flops 2014740352 | bytes 16843392 | tf_op jit(solution)/shard_map/dot_general | solution.py:47
  111.9 40.0 %all-reduce.1 = f32[16,40]{1,0:T(8,128)S(1)} all-reduce(f32[16,40]{1,0:T(8,128)S(1)} %bitcast.64), channel_id=3, replica_groups=mesh['seq'=4,'exp'=2,'hid'=4] {'seq','hid'}, use_global_device_ids=true, to_apply=%region_7.8.clone | all-reduce | flops 640 | bytes 5120
  151.9 0.7 dynamic-slice_bitcast_fusion
  152.6 0.1 select_reduce_fusion
  152.7 0.2 dynamic-update-slice
  153.0 8.5 %all-reduce = bf16[160]{0:T(256)(128)(2,1)S(1)} all-reduce(bf16[160]{0:T(256)(128)(2,1)S(1)} %dynamic-update-slice), channel_id=1, replica_groups=mesh['seq'=4,'exp'=2,'hid'=4] {'seq'}, use_global_device_ids=true, to_apply=%add | all-reduce | flops 160 | bytes 640
  161.5 1.4 multiply_convert_fusion.1
  163.0 9.0 %fusion.15 = f32[4,40,4,1536]{3,1,2,0:T(8,128)S(1)} fusion(bf16[4,40,1024,1]{2,1,3,0:T(8,128)(2,1)S(1)} %bitcast.62, bf16[4,1536,1024,1]{2,1,0,3:T(8,128)(2,1)} %bitcast.59), kind=kOutput, calls=%fused_computation.36 | convolution fusion | flops 2013265920 | bytes 16842752 | tf_op jit(solution)/shard_map/sqf,hcf->shqc/dot_general | solution.py:68
  172.0 10.8 %convolution_add_fusion = f32[4,40,4,1536]{3,1,2,0:T(8,128)} fusion(f32[4,40,4,1536]{3,1,2,0:T(8,128)S(1)} %fusion.15, bf16[4,40,1024,1]{2,1,3,0:T(8,128)(2,1)S(1)} %bitcast.63, bf16[4,1536,1024,1]{2,1,0,3:T(8,128)(2,1)} %bitcast.60), kind=kOutput, calls=%fused_computation.11 | convolution fusion | flops 2014248960 | bytes 20774912 | tf_op jit(solution)/shard_map/sqf,hcf->shqc/dot_general | solution.py:74
  182.9 2.7 psum.15
  185.6 0.6 convert_element_type.76
  186.2 6.6 %convert_bitcast_fusion.1 = bf16[1,6144,1024]{2,1,0:T(8,128)(2,1)} fusion(bf16[160,6144]{1,0:T(8,128)(2,1)S(1)} %copy-done.2, bf16[160,1024]{1,0:T(8,128)(2,1)S(1)} %copy-done.8), kind=kOutput, calls=%fused_computation.7 | convolution fusion | flops 2019557376 | bytes 14876672 | tf_op jit(solution)/shard_map/dot_general | solution.py:63
  192.8 6.6 %convert_bitcast_fusion.2 = bf16[1,6144,1024]{2,1,0:T(8,128)(2,1)} fusion(bf16[160,6144]{1,0:T(8,128)(2,1)S(1)} %copy-done.2, bf16[160,1024]{1,0:T(8,128)(2,1)S(1)} %copy-done.6), kind=kOutput, calls=%fused_computation.8 | convolution fusion | flops 2019557376 | bytes 14876672 | tf_op jit(solution)/shard_map/dot_general | solution.py:60
  199.4 116.0 %reduce-scatter.2.cloned.1.call-done = f32[1,40,1536]{2,1,0:T(8,128)} async-done(((f32[16,40,1536]{2,1,0:T(8,128)}), f32[1,40,1536]{2,1,0:T(8,128)}) %reduce-scatter.2.cloned.1.call-update) | async-done | bytes 245776 | tf_op jit(solution)/shard_map/reduce_scatter | solution.py:86
  315.5 2.5 convolution_convert_fusion.2
  318.0 10.1 %convert_bitcast_fusion = bf16[1,1024,6144]{2,1,0:T(8,128)(2,1)} fusion(bf16[160,6144]{1,0:T(8,128)(2,1)} %all-gather.5.cloned.1.call-done, bf16[160,1024]{1,0:T(8,128)(2,1)} %get-tuple-element.8, f32[160]{0:T(256)S(1)} %convert_element_type.63), kind=kOutput, calls=%fused_computation.6 | convolution fusion | flops 2020048896 | bytes 14877312 | tf_op jit(solution)/shard_map/dot_general | solution.py:52
  328.1 7.9 %all-reduce.4.cloned.1.call-done = bf16[128,1536]{1,0:T(8,128)(2,1)} async-done(((bf16[128,1536]{1,0:T(8,128)(2,1)}), bf16[128,1536]{1,0:T(8,128)(2,1)}) %all-reduce.4.cloned.1.call-update) | async-done | bytes 393232 | tf_op jit(solution)/shard_map/psum | solution.py:96
  336.1 2.0 convert_element_type.74
  (43 shorter events, 0.7 us)
Async XLA Ops:
  7.2 2.1 copy-start
  7.2 5.9 %copy-start.11 = (u32[32]{0:T(128)S(1)}, u32[32]{0:T(128)}, u32[]{:S(2)}) copy-start(u32[32]{0:T(128)} %constant.32) | copy-start | bytes 388
  7.2 6.5 %copy-start.10 = (u32[32]{0:T(128)S(1)}, u32[32]{0:T(128)}, u32[]{:S(2)}) copy-start(u32[32]{0:T(128)} %constant.26) | copy-start | bytes 388
  7.2 49.6 %all-gather.3.cloned.1.call-start = ((), (), s32[]{:S(2)}) async-start(), calls=%async_computation.1 | async-start | bytes 2457600 | tf_op jit(solution)/shard_map/all_gather | solution.py:33
  9.3 5.7 %copy-start.3 = (f32[128,40]{0,1:T(8,128)}, f32[128,40]{0,1:T(8,128)S(1)}, u32[]{:S(2)}) copy-start(f32[128,40]{0,1:T(8,128)S(1)} %convert_reduce_fusion) | copy-start | bytes 61444
  10.4 91.0 %all-gather.5.cloned.1.call-start = ((), (), s32[]{:S(2)}) async-start(), calls=%async_computation.2 | async-start | bytes 2457600 | tf_op jit(solution)/shard_map/all_gather | solution.py:34
  13.0 302.4 %reduce-scatter.2.cloned.1.call-start = ((), (), s32[]{:S(2)}) async-start(), calls=%async_computation.3 | async-start | bytes 4177920 | tf_op jit(solution)/shard_map/reduce_scatter | solution.py:86
  56.8 7.5 %copy-start.2 = (bf16[160,6144]{1,0:T(8,128)(2,1)S(1)}, bf16[160,6144]{1,0:T(8,128)(2,1)}, u32[]{:S(2)}) copy-start(bf16[160,6144]{1,0:T(8,128)(2,1)} %all-gather.3.cloned.1.call-done) | copy-start | bytes 5898244
  71.5 81.1 %copy-start.9 = (f32[128,2]{0,1:T(2,128)S(1)}, f32[128,2]{0,1:T(2,128)}, u32[]{:S(2)}) copy-start(f32[128,2]{0,1:T(2,128)} %param.10) | copy-start | bytes 3076
  163.0 9.0 %copy-start.5 = (bf16[160,1024]{1,0:T(8,128)(2,1)}, bf16[160,1024]{1,0:T(8,128)(2,1)S(1)}, u32[]{:S(2)}) copy-start(bf16[160,1024]{1,0:T(8,128)(2,1)S(1)} %get-tuple-element.12) | copy-start | bytes 983044
  163.0 9.0 %copy-start.7 = (bf16[160,1024]{1,0:T(8,128)(2,1)}, bf16[160,1024]{1,0:T(8,128)(2,1)S(1)}, u32[]{:S(2)}) copy-start(bf16[160,1024]{1,0:T(8,128)(2,1)S(1)} %get-tuple-element.11) | copy-start | bytes 983044
  182.8 3.3 copy-start.8
  182.8 153.2 %all-reduce.4.cloned.1.call-start = ((), (), s32[]{:S(2)}) async-start(), calls=%async_computation.4 | async-start | bytes 786432 | tf_op jit(solution)/shard_map/psum | solution.py:96
  186.2 6.6 %copy-start.6 = (bf16[160,1024]{1,0:T(8,128)(2,1)S(1)}, bf16[160,1024]{1,0:T(8,128)(2,1)}, u32[]{:S(2)}) copy-start(bf16[160,1024]{1,0:T(8,128)(2,1)} %copy-done.5) | copy-start | bytes 983044
  192.8 122.7 %copy-start.4 = (f32[128,40]{0,1:T(8,128)S(1)}, f32[128,40]{0,1:T(8,128)}, u32[]{:S(2)}) copy-start(f32[128,40]{0,1:T(8,128)} %copy-done.3) | copy-start | bytes 61444
  318.0 20.0 %copy-start.1 = (bf16[128,6144]{1,0:T(8,128)(2,1)S(1)}, bf16[128,6144]{1,0:T(8,128)(2,1)}, u32[]{:S(2)}) copy-start(bf16[128,6144]{1,0:T(8,128)(2,1)} %param.7) | copy-start | bytes 4718596
Sparse Core Ops, SparseCore 0:
  10.5 46.2 all-gather.2
  59.0 42.3 all-gather.4
  183.0 132.4 reduce-scatter.1
  318.2 17.7 all-reduce.3
where the time goes:
time: 345 us
  waiting for transfers between devices  196 us (57%)
  matrix products  74.3 us (22%)
  blocking collectives  51.3 us (15%)
  between operations  14.6 us (4%)
  other arithmetic  5.25 us (2%)
    reduce_scatter x1, waiting for transfers between devices, on_device(): lax.psum_scatter(flat_parts, ('seq', 'hid'), scatter_dimension=0, tiled=T...  116 us
    unnamed x2, blocking collectives  48.6 us
    all_gather x1, waiting for transfers between devices, on_device(): lax.all_gather(token_slots, 'seq', axis=0, tiled=True)  41.9 us
    all_gather x1, waiting for transfers between devices, on_device(): lax.all_gather(grad_slots, 'seq', axis=0, tiled=True)  29.9 us
    dot_general x1, matrix products, on_device(): jnp.einsum('sqf,hcf->shqc', up_blocks, up_mat.reshape(hid_count, piece_wi...  10.8 us
    dot_general x1, matrix products, on_device(): lax.dot_general(grads_e, down_mat, (((1,), (1,)), ((), ())), preferred_el...  10.4 us
    dot_general x1, matrix products, on_device(): lax.dot_general(weighted, grads_e, contract_rows, preferred_element_type=...  10.1 us
    dot_general x1, matrix products, on_device(): jnp.einsum('sqf,hcf->shqc', gate_blocks, gate_mat.reshape(hid_count, piec...  9.01 us
  transfers between devices with their start and end apart: 4, of which 4 were waited for; matrix products, arithmetic and copies ran while one was open for 12% of the time, Pallas kernels for 0%

commit v1 on v0

--- a/solution.py
+++ b/solution.py
@@ -29,8 +29,33 @@
         select_half, out_grad, contract_rows, preferred_element_type=jnp.float32
     ).astype(jnp.bfloat16)
     weight_slots = jnp.sum(pick_table * gate_probs[:, :, None], axis=(0, 1))
+
+    def trails_connect(q_in):
+        piece_now, r1, long_array = (lax.axis_size("seq"), lax.axis_index("seq"), q_in.shape[0])
+        shelf = []
+        for it in [*range(piece_now)]:
+            shelf.append((it, (it + 1) % piece_now))
+        in_order = []
+        for it in [*range(piece_now)]:
+            in_order.append((it, (it - 1) % piece_now))
+        a_now = jnp.zeros((*q_in.shape[:0], piece_now * long_array, *q_in.shape[1:]), q_in.dtype)
+        a_now = lax.dynamic_update_slice_in_dim(a_now, q_in, r1 * long_array, axis=0)
+        w1 = aux = q_in
+        block_next = piece_now // 2
+        for s in tuple(range(1, block_next + 1)):
+            w1 = lax.ppermute(w1, axis_name="seq", perm=shelf)
+            a_now = lax.dynamic_update_slice_in_dim(
+                a_now, w1, (r1 - s) % piece_now * long_array, axis=0
+            )
+            if s < piece_now - block_next:
+                aux = lax.ppermute(aux, axis_name="seq", perm=in_order)
+                a_now = lax.dynamic_update_slice_in_dim(
+                    a_now, aux, (r1 + s) % piece_now * long_array, axis=0
+                )
+        return a_now
+
     rows_e, grads_e, weight_e = (
-        lax.all_gather(token_slots, "seq", axis=0, tiled=True),
+        trails_connect(token_slots),
         lax.all_gather(grad_slots, "seq", axis=0, tiled=True),
         lax.all_gather(weight_slots.astype(jnp.bfloat16), "seq", axis=0, tiled=True).astype(
             weight_slots.dtype

time: 345 us -> 326 us (0.945)
  waiting for transfers between devices: 196 us -> 176 us
  matrix products: 74.3 us -> 67.4 us
  starting transfers between devices: 0.16 us -> 5.65 us
    ppermute x0 -> x3, waiting for transfers between devices: none -> 48.9 us  [the longest x1 38.1 us: trails_connect(): aux = lax.ppermute(aux, axis_name='seq', perm=in_order)]
    all_gather x1 -> x0, waiting for transfers between devices: 41.9 us -> none  [on_device(): lax.all_gather(token_slots, 'seq', axis=0, tiled=True)]
    all_gather x1, waiting for transfers between devices: 29.9 us -> 2.64 us  [on_device(): lax.all_gather(grad_slots, 'seq', axis=0, tiled=True)]
    ppermute x0 -> x3, starting transfers between devices: none -> 5.53 us  [the longest x2 3.5 us: trails_connect(): w1 = lax.ppermute(w1, axis_name='seq', perm=shelf)]
    dot_general x1, matrix products: 7.11 us -> 2.19 us  [on_device(): up_pre = jnp.dot(rows_e, up_mat, preferred_element_type=jnp.float32)]
  transfers between devices with their start and end apart: 4 -> 6, of which waited for: 4 -> 6; matrix products, arithmetic and copies ran while one was open for 12% -> 11% of each run, Pallas kernels for 0% -> 0%
where the time goes in v1:
time: 326 us; the launch traced here: 325 us
  waiting for transfers between devices  176 us (54%)
  matrix products  67.4 us (21%)
  blocking collectives  52.9 us (16%)
  between operations  14.7 us (5%)
  starting transfers between devices  5.65 us (2%)
  other arithmetic  5.26 us (2%)
  local copies, waits for them, and re-layouts  3.47 us (1%)
    reduce_scatter x1, waiting for transfers between devices, on_device(): lax.psum_scatter(flat_parts, ('seq', 'hid'), scatter_dimension=0, tiled=T...  116 us
    unnamed x2, blocking collectives  50.2 us
    ppermute x1, waiting for transfers between devices, trails_connect(): aux = lax.ppermute(aux, axis_name='seq', perm=in_order)  38.1 us
    dot_general x1, matrix products, on_device(): jnp.einsum('sqf,hcf->shqc', up_blocks, up_mat.reshape(hid_count, piece_wi...  10.8 us
    ppermute x2, waiting for transfers between devices, trails_connect(): w1 = lax.ppermute(w1, axis_name='seq', perm=shelf)  10.8 us
    dot_general x1, matrix products, on_device(): lax.dot_general(grads_e, down_mat, (((1,), (1,)), ((), ())), preferred_el...  10.4 us
    dot_general x1, matrix products, on_device(): lax.dot_general(weighted, grads_e, contract_rows, preferred_element_type=...  10.1 us
    dot_general x1, matrix products, on_device(): jnp.einsum('sqf,hcf->shqc', gate_blocks, gate_mat.reshape(hid_count, piec...  9.01 us
  transfers between devices with their start and end apart: 6, of which 6 were waited for; matrix products, arithmetic and copies ran while one was open for 11% of the time, Pallas kernels for 0%

profile of v1, /device:TPU:0, one launch (start us, length us, event | category | flops | bytes accessed | tf_op | source)
XLA Modules:
  0.0 325.2 jit_solution(1377726241596858932)
XLA Ops:
  7.2 0.8 broadcast_compare_fusion
  8.3 0.3 reduce-window.9
  9.5 1.1 constant_dynamic-update-slice_fusion.3
  10.6 3.0 collective-permute-start
  13.6 2.0 collective-permute-start.1
  15.7 1.1 convolution_convert_fusion
  16.9 0.6 dynamic-slice.1
  17.5 0.6 dynamic-slice
  18.8 9.2 %collective-permute-done = bf16[40,6144]{1,0:T(8,128)(2,1)S(1)} collective-permute-done((bf16[40,6144]{1,0:T(8,128)(2,1)}, bf16[40,6144]{1,0:T(8,128)(2,1)S(1)}, u32[]{:S(2)}, u32[]{:S(2)}) %collective-permute-start) | collective-permute-done | bytes 491552 | tf_op jit(solution)/shard_map/ppermute | solution.py:46
  28.0 0.5 collective-permute-start.2
  28.5 38.1 %collective-permute-done.1 = bf16[40,6144]{1,0:T(8,128)(2,1)S(1)} collective-permute-done((bf16[40,6144]{1,0:T(8,128)(2,1)}, bf16[40,6144]{1,0:T(8,128)(2,1)S(1)}, u32[]{:S(2)}, u32[]{:S(2)}) %collective-permute-start.1) | collective-permute-done | bytes 491552 | tf_op jit(solution)/shard_map/ppermute | solution.py:51
  66.7 1.6 collective-permute-done.2
  68.3 6.9 %fusion = f32[160,1024]{1,0:T(8,128)S(1)} fusion(bf16[160,6144]{1,0:T(8,128)(2,1)S(1)} %constant_dynamic-update-slice_fusion, bf16[1,6144,1024]{2,1,0:T(8,128)(2,1)} %param.11), kind=kOutput, calls=%fused_computation | convolution fusion | flops 2013265920 | bytes 15204352 | tf_op jit(solution)/shard_map/dot_general | solution.py:67
  75.4 2.2 fusion.2
  77.6 2.6 all-gather.2.cloned.1.call-done
  80.3 10.4 %fusion.7 = (f32[160]{0:T(256)S(1)}, bf16[160,1024]{1,0:T(8,128)(2,1)}, f32[160,1024]{1,0:T(8,128)}) fusion(f32[160,1024]{1,0:T(8,128)S(1)} %fusion.2, f32[160,1024]{1,0:T(8,128)S(1)} %fusion, bf16[160,6144]{1,0:T(8,128)(2,1)} %all-gather.2.cloned.1.call-done, bf16[1,1024,6144]{2,1,0:T(8,128)(2,1)} %param.13), kind=kOutput, calls=%fused_computation.16 | convolution fusion | flops 2014740352 | bytes 16843392 | tf_op jit(solution)/shard_map/dot_general | solution.py:72
  90.7 41.7 %all-reduce.1 = f32[16,40]{1,0:T(8,128)S(1)} all-reduce(f32[16,40]{1,0:T(8,128)S(1)} %bitcast.66), channel_id=3, replica_groups=mesh['seq'=4,'exp'=2,'hid'=4] {'seq','hid'}, use_global_device_ids=true, to_apply=%region_7.8.clone | all-reduce | flops 640 | bytes 5120
  132.4 0.7 dynamic-slice_bitcast_fusion
  133.2 0.2 dynamic-update-slice
  133.5 8.5 %all-reduce = bf16[160]{0:T(256)(128)(2,1)S(1)} all-reduce(bf16[160]{0:T(256)(128)(2,1)S(1)} %dynamic-update-slice), channel_id=1, replica_groups=mesh['seq'=4,'exp'=2,'hid'=4] {'seq'}, use_global_device_ids=true, to_apply=%add | all-reduce | flops 160 | bytes 640
  142.0 1.4 multiply_convert_fusion.1
  143.5 9.0 %fusion.15 = f32[4,40,4,1536]{3,1,2,0:T(8,128)S(1)} fusion(bf16[4,40,1024,1]{2,1,3,0:T(8,128)(2,1)S(1)} %bitcast.64, bf16[4,1536,1024,1]{2,1,0,3:T(8,128)(2,1)} %bitcast.59), kind=kOutput, calls=%fused_computation.40 | convolution fusion | flops 2013265920 | bytes 16842752 | tf_op jit(solution)/shard_map/sqf,hcf->shqc/dot_general | solution.py:93
  152.5 10.8 %convolution_add_fusion = f32[4,40,4,1536]{3,1,2,0:T(8,128)} fusion(f32[4,40,4,1536]{3,1,2,0:T(8,128)S(1)} %fusion.15, bf16[4,40,1024,1]{2,1,3,0:T(8,128)(2,1)S(1)} %bitcast.65, bf16[4,1536,1024,1]{2,1,0,3:T(8,128)(2,1)} %bitcast.60), kind=kOutput, calls=%fused_computation.11 | convolution fusion | flops 2014248960 | bytes 20774912 | tf_op jit(solution)/shard_map/sqf,hcf->shqc/dot_general | solution.py:99
  163.4 2.7 psum.15
  166.1 0.6 convert_element_type.76
  166.6 6.6 %convert_bitcast_fusion.1 = bf16[1,6144,1024]{2,1,0:T(8,128)(2,1)} fusion(bf16[160,6144]{1,0:T(8,128)(2,1)S(1)} %constant_dynamic-update-slice_fusion, bf16[160,1024]{1,0:T(8,128)(2,1)S(1)} %copy-done.8), kind=kOutput, calls=%fused_computation.7 | convolution fusion | flops 2019557376 | bytes 14876672 | tf_op jit(solution)/shard_map/dot_general | solution.py:88
  173.3 6.6 %convert_bitcast_fusion.2 = bf16[1,6144,1024]{2,1,0:T(8,128)(2,1)} fusion(bf16[160,6144]{1,0:T(8,128)(2,1)S(1)} %constant_dynamic-update-slice_fusion, bf16[160,1024]{1,0:T(8,128)(2,1)S(1)} %copy-done.6), kind=kOutput, calls=%fused_computation.8 | convolution fusion | flops 2019557376 | bytes 14876672 | tf_op jit(solution)/shard_map/dot_general | solution.py:85
  179.9 116.2 %reduce-scatter.2.cloned.1.call-done = f32[1,40,1536]{2,1,0:T(8,128)} async-done(((f32[16,40,1536]{2,1,0:T(8,128)}), f32[1,40,1536]{2,1,0:T(8,128)}) %reduce-scatter.2.cloned.1.call-update) | async-done | bytes 245776 | tf_op jit(solution)/shard_map/reduce_scatter | solution.py:111
  296.1 2.5 convolution_convert_fusion.2
  298.7 10.1 %convert_bitcast_fusion = bf16[1,1024,6144]{2,1,0:T(8,128)(2,1)} fusion(bf16[160,6144]{1,0:T(8,128)(2,1)} %all-gather.2.cloned.1.call-done, bf16[160,1024]{1,0:T(8,128)(2,1)} %get-tuple-element.8, f32[160]{0:T(256)S(1)} %convert_element_type.63), kind=kOutput, calls=%fused_computation.6 | convolution fusion | flops 2020048896 | bytes 14877312 | tf_op jit(solution)/shard_map/dot_general | solution.py:77
  308.8 8.0 %all-reduce.4.cloned.1.call-done = bf16[128,1536]{1,0:T(8,128)(2,1)} async-done(((bf16[128,1536]{1,0:T(8,128)(2,1)}), bf16[128,1536]{1,0:T(8,128)(2,1)}) %all-reduce.4.cloned.1.call-update) | async-done | bytes 393232 | tf_op jit(solution)/shard_map/psum | solution.py:121
  316.7 2.0 convert_element_type.74
  (57 shorter events, 1.8 us)
Async XLA Ops:
  7.2 2.3 copy-start
  7.2 73.1 %all-gather.2.cloned.1.call-start = ((), (), s32[]{:S(2)}) async-start(), calls=%async_computation.1 | async-start | bytes 2457600 | tf_op jit(solution)/shard_map/all_gather | solution.py:59
  9.2 6.4 %copy-start.3 = (f32[128,40]{0,1:T(8,128)}, f32[128,40]{0,1:T(8,128)S(1)}, u32[]{:S(2)}) copy-start(f32[128,40]{0,1:T(8,128)S(1)} %convert_reduce_fusion) | copy-start | bytes 61444
  9.2 6.4 %copy-start.2 = (bf16[128,6144]{1,0:T(8,128)(2,1)S(1)}, bf16[128,6144]{1,0:T(8,128)(2,1)}, u32[]{:S(2)}) copy-start(bf16[128,6144]{1,0:T(8,128)(2,1)} %param.8) | copy-start | bytes 4718596
  10.6 6.3 %copy-start.11 = (u32[32]{0:T(128)S(1)}, u32[32]{0:T(128)}, u32[]{:S(2)}) copy-start(u32[32]{0:T(128)} %constant.68) | copy-start | bytes 388
  10.6 6.9 %copy-start.10 = (u32[32]{0:T(128)S(1)}, u32[32]{0:T(128)}, u32[]{:S(2)}) copy-start(u32[32]{0:T(128)} %constant.62) | copy-start | bytes 388
  10.6 17.4 %collective-permute-start = (bf16[40,6144]{1,0:T(8,128)(2,1)}, bf16[40,6144]{1,0:T(8,128)(2,1)S(1)}, u32[]{:S(2)}, u32[]{:S(2)}) collective-permute-start(bf16[40,6144]{1,0:T(8,128)(2,1)} %get-tuple-element.14), channel_id=1, source_target_pairs={{0,8},{8,16},{16,24},{24,0},{1,9},{9,17},{17,25},{25,1},{2,10},{10... | collective-permute-start | bytes 1474568 | tf_op jit(solution)/shard_map/ppermute | solution.py:46
  13.6 53.0 %collective-permute-start.1 = (bf16[40,6144]{1,0:T(8,128)(2,1)}, bf16[40,6144]{1,0:T(8,128)(2,1)S(1)}, u32[]{:S(2)}, u32[]{:S(2)}) collective-permute-start(bf16[40,6144]{1,0:T(8,128)(2,1)} %get-tuple-element.14), channel_id=1, source_target_pairs={{0,24},{8,0},{16,8},{24,16},{1,25},{9,1},{17,9},{25,17},{2,26},{10... | collective-permute-start | bytes 1474568 | tf_op jit(solution)/shard_map/ppermute | solution.py:51
  16.8 279.3 %reduce-scatter.2.cloned.1.call-start = ((), (), s32[]{:S(2)}) async-start(), calls=%async_computation.2 | async-start | bytes 4177920 | tf_op jit(solution)/shard_map/reduce_scatter | solution.py:111
  28.0 40.3 %collective-permute-start.2 = (bf16[40,6144]{1,0:T(8,128)(2,1)S(1)}, bf16[40,6144]{1,0:T(8,128)(2,1)S(1)}, u32[]{:S(2)}, u32[]{:S(2)}) collective-permute-start(bf16[40,6144]{1,0:T(8,128)(2,1)S(1)} %collective-permute-done), channel_id=1, source_target_pairs={{0,8},{8,16},{16,24},{24,0},{1,9},{9,17},{17,25},{25,1},{2,10},{10... | collective-permute-start | bytes 1474568 | tf_op jit(solution)/shard_map/ppermute | solution.py:46
  66.6 8.6 %slice-start = ((s8[12582912]{0:T(1024)(128)(4,1)}), s8[4194304]{0:T(1024)(128)(4,1)S(1)}, s32[]{:S(2)}) async-start(s8[12582912]{0:T(1024)(128)(4,1)} %bitcast.61), calls=%async_computation.4 | async-start | bytes 8388608
  68.3 7.0 %slice-start.1 = ((s8[12582912]{0:T(1024)(128)(4,1)}), s8[4194304]{0:T(1024)(128)(4,1)S(1)}, s32[]{:S(2)}) async-start(s8[12582912]{0:T(1024)(128)(4,1)} %bitcast.61), calls=%async_computation.5 | async-start | bytes 8388608
  68.3 7.1 %slice-start.2 = ((s8[12582912]{0:T(1024)(128)(4,1)}), s8[4194304]{0:T(1024)(128)(4,1)S(1)}, s32[]{:S(2)}) async-start(s8[12582912]{0:T(1024)(128)(4,1)} %bitcast.61), calls=%async_computation.6 | async-start | bytes 8388608
  77.6 55.5 %copy-start.9 = (f32[128,2]{0,1:T(2,128)S(1)}, f32[128,2]{0,1:T(2,128)}, u32[]{:S(2)}) copy-start(f32[128,2]{0,1:T(2,128)} %param.10) | copy-start | bytes 3076
  143.4 9.0 %copy-start.5 = (bf16[160,1024]{1,0:T(8,128)(2,1)}, bf16[160,1024]{1,0:T(8,128)(2,1)S(1)}, u32[]{:S(2)}) copy-start(bf16[160,1024]{1,0:T(8,128)(2,1)S(1)} %get-tuple-element.12) | copy-start | bytes 983044
  143.5 9.0 %copy-start.7 = (bf16[160,1024]{1,0:T(8,128)(2,1)}, bf16[160,1024]{1,0:T(8,128)(2,1)S(1)}, u32[]{:S(2)}) copy-start(bf16[160,1024]{1,0:T(8,128)(2,1)S(1)} %get-tuple-element.11) | copy-start | bytes 983044
  163.3 3.3 %copy-start.8 = (bf16[160,1024]{1,0:T(8,128)(2,1)S(1)}, bf16[160,1024]{1,0:T(8,128)(2,1)}, u32[]{:S(2)}) copy-start(bf16[160,1024]{1,0:T(8,128)(2,1)} %copy-done.7) | copy-start | bytes 983044
  163.3 153.4 %all-reduce.4.cloned.1.call-start = ((), (), s32[]{:S(2)}) async-start(), calls=%async_computation.3 | async-start | bytes 786432 | tf_op jit(solution)/shard_map/psum | solution.py:121
  166.6 6.6 %copy-start.6 = (bf16[160,1024]{1,0:T(8,128)(2,1)S(1)}, bf16[160,1024]{1,0:T(8,128)(2,1)}, u32[]{:S(2)}) copy-start(bf16[160,1024]{1,0:T(8,128)(2,1)} %copy-done.5) | copy-start | bytes 983044
  173.3 122.8 %copy-start.4 = (f32[128,40]{0,1:T(8,128)S(1)}, f32[128,40]{0,1:T(8,128)}, u32[]{:S(2)}) copy-start(f32[128,40]{0,1:T(8,128)} %copy-done.3) | copy-start | bytes 61444
  298.7 20.0 %copy-start.1 = (bf16[128,6144]{1,0:T(8,128)(2,1)S(1)}, bf16[128,6144]{1,0:T(8,128)(2,1)}, u32[]{:S(2)}) copy-start(bf16[128,6144]{1,0:T(8,128)(2,1)} %param.7) | copy-start | bytes 4718596
Sparse Core Ops, SparseCore 0:
  16.9 63.2 all-gather.1
  163.5 132.6 reduce-scatter.1
  299.0 17.6 all-reduce.3
